TPU v7x, 32 devices: a whole 2x2x4 slice. The times are simulated.
32 devices in a mesh: dp: 8 (over y, x, core), tensor: 4 (over z).
Axes of the slice: x: 2, y: 2, z: 4, core: 2. Of those that a mesh axis runs over, the one named last changes fastest.
Arguments:
- tokens: bfloat16 [16384, 1536], P('dp'), may hold values from -6 to 6
- cotangent: bfloat16 [16384, 1536], P('dp'), may hold values from -6 to 6
- destination: int32 [16384], P('dp'), may hold values from 0 to 16383, as said below
- lengths: int32 [8, 4], P('dp'), may hold values from 1 to 1024, 2048 in all within a row
- norm_gain: float32 [1536], replicated, may hold values from 0.1 to 1.9
- inner_weight: float32 [1536, 2, 3072], P('dp', None, 'tensor'), may hold values from -0.15625 to 0.15625
- shared_weight: float32 [1536, 256], P('dp'), may hold values from -0.15625 to 0.15625
- step_weight: float32 [1536, 48], P('dp', 'tensor'), may hold values from -0.15625 to 0.15625
- filter_weight: float32 [4, 3072], P(None, 'tensor'), may hold values from -3 to 3
- filter_bias: float32 [3072], P('tensor'), may hold values from -3 to 3
- shared_filter: float32 [4, 256], replicated, may hold values from -3 to 3
- shared_filter_bias: float32 [256], replicated, may hold values from -3 to 3
- step_bias: float32 [48], P('tensor'), may hold values from -6 to -2
- decay_log: float32 [48], P('tensor'), may hold values from 0 to 2.77
- skip_gain: float32 [48], P('tensor'), may hold values from 0.5 to 1.5
- gate_gain: float32 [3072], P('tensor'), may hold values from 0.1 to 1.9
- out_weight: float32 [1536, 3072], P('dp', 'tensor'), may hold values from -0.109375 to 0.109375
Outputs:
- layer_out: bfloat16 [16384, 1536], P('dp')
- input_grad: bfloat16 [16384, 1536], P('dp')
- norm_gain_grad: float32 [1536], replicated
- inner_weight_grad: float32 [1536, 2, 3072], P('dp', None, 'tensor')
- shared_weight_grad: float32 [1536, 256], P('dp')
- step_weight_grad: float32 [1536, 48], P('dp', 'tensor')
- filter_weight_grad: float32 [4, 3072], P(None, 'tensor')
- filter_bias_grad: float32 [3072], P('tensor')
- shared_filter_grad: float32 [4, 256], replicated
- shared_filter_bias_grad: float32 [256], replicated
- step_bias_grad: float32 [48], P('tensor')
- decay_log_grad: float32 [48], P('tensor')
- skip_gain_grad: float32 [48], P('tensor')
- gate_gain_grad: float32 [3072], P('tensor')
- out_weight_grad: float32 [1536, 3072], P('dp', 'tensor')
Inputs may be any that keep to these rules, and one draw needn't show every extreme that they name: destination is a permutation. The tokens at given positions s * 2048 to (s + 1) * 2048 - 1 that go to work block w take exactly the work positions w * 2048 + s * 256 to w * 2048 + (s + 1) * 256 - 1. `lengths`: each row sums to 2048, and its longest sequence has exactly 1024 tokens.
All inputs are finite; a program needn't handle non-finite values.
Results may differ from a plain program's by a relative error of at most 0.012.
Values may be sent and summed in bfloat16 or wider, within the bound.
No kernel may reach another device: no remote copies, remote signals or barrier semaphores. Data moves between devices by JAX's collectives and lax.ppermute only.
A program may use at most 256 MiB of HBM per device.

v0:
```python
import jax
import jax.numpy as jnp
from jax import lax
from jax.sharding import PartitionSpec as P

INNER = 3072
SPAN = 256
EPSILON = 1e-05
PRECISE = lax.Precision.HIGHEST


def segments_of(lengths, row_count):
    seq_ends = jnp.cumsum(lengths)
    seq_starts = seq_ends - lengths
    places = jnp.arange(row_count, dtype=jnp.int32)
    segment = jnp.sum((places[:, None] >= seq_ends[None, :]).astype(jnp.int32), axis=1)
    belongs = segment[:, None] == jnp.arange(lengths.shape[0], dtype=jnp.int32)[None, :]
    position = places - jnp.sum(jnp.where(belongs, seq_starts[None, :], 0), axis=1)
    return (segment, position)


def causal_filter(signal, kernel, offset_bias, position):
    result = offset_bias + kernel[0] * signal
    for offset in range(1, kernel.shape[0]):
        shifted = jnp.pad(signal, ((offset, 0), (0, 0)))[: signal.shape[0]]
        allowed = (position >= offset).astype(signal.dtype)
        result = result + kernel[offset] * shifted * allowed[:, None]
    return result


def mixer(
    inputs,
    shared,
    step_raw,
    filter_weight,
    filter_bias,
    shared_filter,
    shared_filter_bias,
    step_bias,
    decay_log,
    skip_gain,
    segment,
    position,
):
    row_count = inputs.shape[0]
    heads_here = step_bias.shape[0]
    state_size = shared.shape[1] // 2
    values = jax.nn.silu(causal_filter(inputs, filter_weight, filter_bias, position)).reshape(
        row_count, heads_here, -1
    )
    factors = jax.nn.silu(causal_filter(shared, shared_filter, shared_filter_bias, position))
    writes = factors[:, :state_size]
    read_vectors = factors[:, state_size:]
    step_size = jax.nn.softplus(step_raw + step_bias)
    log_decay = -step_size * jnp.exp(decay_log)
    blocks = row_count // SPAN
    causal = jnp.arange(SPAN)[:, None] >= jnp.arange(SPAN)[None, :]

    def blocked(whole_array):
        return whole_array.reshape((blocks, SPAN) + whole_array.shape[1:])

    def span_step(state_carry, block_item):
        memory, last_segment = state_carry
        value_blk, write_blk, read_blk, size_blk, decay_blk, segment_blk = block_item
        cumulative = jnp.cumsum(decay_blk, axis=0).T
        inside = causal & (segment_blk[:, None] == segment_blk[None, :])
        spread = cumulative[:, :, None] - cumulative[:, None, :]
        decays = jnp.exp(jnp.where(inside[None], spread, -jnp.inf))
        scores = jnp.dot(read_blk, write_blk.T, precision=PRECISE)
        mixing = scores[None] * decays * size_blk.T[:, None, :]
        local_out = jnp.einsum("hts,shp->thp", mixing, value_blk, precision=PRECISE)
        carried = (segment_blk == last_segment).astype(value_blk.dtype)
        entering = jnp.exp(cumulative).T * carried[:, None]
        remote_out = (
            jnp.einsum("tn,hnp->thp", read_blk, memory, precision=PRECISE) * entering[:, :, None]
        )
        block_out = local_out + remote_out + skip_gain[None, :, None] * value_blk
        end_segment = segment_blk[-1]
        closing = (segment_blk == end_segment).astype(value_blk.dtype)
        weights = jnp.exp(cumulative[:, -1:] - cumulative) * size_blk.T * closing[None, :]
        added_state = jnp.einsum("sn,hs,shp->hnp", write_blk, weights, value_blk, precision=PRECISE)
        keeping = jnp.exp(cumulative[:, -1]) * (last_segment == end_segment).astype(value_blk.dtype)
        memory = memory * keeping[:, None, None] + added_state
        return ((memory, end_segment), block_out)

    initial = (jnp.zeros((heads_here, state_size, values.shape[2]), values.dtype), jnp.int32(-1))
    unused, outputs = lax.scan(
        jax.checkpoint(span_step),
        initial,
        (
            blocked(values),
            blocked(writes),
            blocked(read_vectors),
            blocked(step_size),
            blocked(log_decay),
            blocked(segment),
        ),
    )
    return outputs.reshape(row_count, -1)


def prenorm(hidden_in, norm_gain):
    scale = lax.rsqrt(jnp.mean(hidden_in * hidden_in, axis=1, keepdims=True) + EPSILON)
    return hidden_in * scale * norm_gain


def on_device(
    tokens,
    cotangent,
    destination,
    lengths,
    norm_gain,
    inner_weight,
    shared_weight,
    step_weight,
    filter_weight,
    filter_bias,
    shared_filter,
    shared_filter_bias,
    step_bias,
    decay_log,
    skip_gain,
    gate_gain,
    out_weight,
):
    row_count = tokens.shape[0]
    model_width = tokens.shape[1]
    group_rows = row_count // lax.axis_size("dp")
    my_index = lax.axis_index("dp")
    target_block = destination // row_count
    send_slot = (
        target_block * group_rows + (destination - target_block * row_count) - my_index * group_rows
    )
    send_order = (
        jnp.zeros((row_count,), jnp.int32).at[send_slot].set(jnp.arange(row_count, dtype=jnp.int32))
    )
    send_tokens = tokens[send_order]
    send_cot = cotangent[send_order]
    work_tokens, work_cot = (
        lax.all_to_all(send_tokens, "dp", split_axis=0, concat_axis=0, tiled=True),
        lax.all_to_all(send_cot, "dp", split_axis=0, concat_axis=0, tiled=True),
    )
    inner_full, shared_full, step_full, out_full = (
        lax.all_gather(inner_weight.astype(jnp.bfloat16), "dp", axis=0, tiled=True),
        lax.all_gather(shared_weight.astype(jnp.bfloat16), "dp", axis=0, tiled=True),
        lax.all_gather(step_weight.astype(jnp.bfloat16), "dp", axis=0, tiled=True),
        lax.all_gather(out_weight.astype(jnp.bfloat16), "dp", axis=0, tiled=True),
    )
    col_share = model_width // lax.axis_size("tensor")
    column = lax.axis_index("tensor") * col_share
    hidden_in = work_tokens.astype(jnp.float32)
    segment, position = segments_of(lengths[0], row_count)
    normed, pull_norm = jax.vjp(prenorm, hidden_in, norm_gain)
    normed_low = normed.astype(jnp.bfloat16)
    inner_flat = inner_full.reshape(inner_full.shape[0], -1)
    both = jnp.dot(normed_low, inner_flat, preferred_element_type=jnp.float32)
    half_width = both.shape[1] // 2
    gate_in = both[:, :half_width]
    inputs = both[:, half_width:]
    shared = jnp.dot(normed_low, shared_full, preferred_element_type=jnp.float32)
    step_raw = jnp.dot(normed_low, step_full, preferred_element_type=jnp.float32)

    def local_mixer(
        inputs,
        shared,
        step_raw,
        filter_weight,
        filter_bias,
        shared_filter,
        shared_filter_bias,
        step_bias,
        decay_log,
        skip_gain,
    ):
        return mixer(
            inputs,
            shared,
            step_raw,
            filter_weight,
            filter_bias,
            shared_filter,
            shared_filter_bias,
            step_bias,
            decay_log,
            skip_gain,
            segment,
            position,
        )

    mixed_in, pull_mixer = jax.vjp(
        local_mixer,
        inputs,
        shared,
        step_raw,
        filter_weight,
        filter_bias,
        shared_filter,
        shared_filter_bias,
        step_bias,
        decay_log,
        skip_gain,
    )
    gate_sig = jax.nn.sigmoid(gate_in)
    gate_act = gate_in * gate_sig
    gated = mixed_in * gate_act
    square_sum = lax.psum(jnp.sum(gated * gated, axis=1), "tensor")
    gate_scale = lax.rsqrt(square_sum / INNER + EPSILON)[:, None]
    gate_normed = (gated * gate_scale * gate_gain).astype(jnp.bfloat16)
    partial_out = jnp.einsum("ti,di->td", gate_normed, out_full, preferred_element_type=jnp.float32)
    branch = lax.psum(partial_out, "tensor")
    layer_work = (hidden_in + branch).astype(jnp.bfloat16)
    part_out = lax.dynamic_slice_in_dim(layer_work, column, col_share, 1)
    out_grad = jnp.einsum("td,ti->di", work_cot, gate_normed, preferred_element_type=jnp.float32)
    normed_grad = jnp.einsum("td,di->ti", work_cot, out_full, preferred_element_type=jnp.float32)
    gate_gain_grad = jnp.sum(normed_grad * gated * gate_scale, axis=0)
    scaled_grad = normed_grad * gate_gain
    cross_sum = lax.psum(jnp.sum(scaled_grad * gated, axis=1), "tensor")
    gated_grad = gate_scale * scaled_grad - gated * gate_scale**3 * (cross_sum / INNER)[:, None]
    mixed_grad = gated_grad * gate_act
    gate_in_grad = gated_grad * mixed_in * gate_sig * (1.0 + gate_in * (1.0 - gate_sig))
    (
        inputs_grad,
        shared_part,
        step_raw_grad,
        filter_weight_grad,
        filter_bias_grad,
        shared_filter_part,
        shared_bias_part,
        step_bias_grad,
        decay_log_grad,
        skip_gain_grad,
    ) = pull_mixer(mixed_grad)
    shared_grad, shared_filter_grad, shared_filter_bias_grad = lax.psum(
        (shared_part, shared_filter_part, shared_bias_part), "tensor"
    )
    both_low = jnp.concatenate([gate_in_grad, inputs_grad], axis=1).astype(jnp.bfloat16)
    shared_low = shared_grad.astype(jnp.bfloat16)
    step_low = step_raw_grad.astype(jnp.bfloat16)
    input_part = jnp.einsum("tk,dk->td", both_low, inner_flat, preferred_element_type=jnp.float32)
    input_part = input_part + jnp.einsum(
        "tk,dk->td", step_low, step_full, preferred_element_type=jnp.float32
    )
    normed_back = lax.psum(input_part, "tensor")
    normed_back = normed_back + jnp.einsum(
        "tk,dk->td", shared_low, shared_full, preferred_element_type=jnp.float32
    )
    input_norm_grad, norm_gain_grad = pull_norm(normed_back)
    input_work = (input_norm_grad + work_cot.astype(jnp.float32)).astype(jnp.bfloat16)
    part_grad = lax.dynamic_slice_in_dim(input_work, column, col_share, 1)
    inner_grad = jnp.einsum(
        "td,tk->dk", normed_low, both_low, preferred_element_type=jnp.float32
    ).reshape(inner_full.shape)
    shared_weight_grad = jnp.einsum(
        "td,tk->dk", normed_low, shared_low, preferred_element_type=jnp.float32
    )
    step_weight_grad = jnp.einsum(
        "td,tk->dk", normed_low, step_low, preferred_element_type=jnp.float32
    )
    inner_grad, shared_weight_grad, step_weight_grad, out_grad = (
        lax.psum_scatter(inner_grad, "dp", scatter_dimension=0, tiled=True),
        lax.psum_scatter(shared_weight_grad, "dp", scatter_dimension=0, tiled=True),
        lax.psum_scatter(step_weight_grad, "dp", scatter_dimension=0, tiled=True),
        lax.psum_scatter(out_grad, "dp", scatter_dimension=0, tiled=True),
    )
    (
        norm_gain_grad,
        filter_weight_grad,
        filter_bias_grad,
        shared_filter_grad,
        shared_filter_bias_grad,
        step_bias_grad,
        decay_log_grad,
        skip_gain_grad,
        gate_gain_grad,
    ) = lax.psum(
        (
            norm_gain_grad,
            filter_weight_grad,
            filter_bias_grad,
            shared_filter_grad,
            shared_filter_bias_grad,
            step_bias_grad,
            decay_log_grad,
            skip_gain_grad,
            gate_gain_grad,
        ),
        "dp",
    )
    part_out, part_grad = (
        lax.all_to_all(part_out, "dp", split_axis=0, concat_axis=0, tiled=True),
        lax.all_to_all(part_grad, "dp", split_axis=0, concat_axis=0, tiled=True),
    )
    back_out, back_grad = (
        lax.all_gather(part_out, "tensor", axis=1, tiled=True),
        lax.all_gather(part_grad, "tensor", axis=1, tiled=True),
    )
    layer_out = back_out[send_slot]
    input_grad = back_grad[send_slot]
    return (
        layer_out,
        input_grad,
        norm_gain_grad,
        inner_grad,
        shared_weight_grad,
        step_weight_grad,
        filter_weight_grad,
        filter_bias_grad,
        shared_filter_grad,
        shared_filter_bias_grad,
        step_bias_grad,
        decay_log_grad,
        skip_gain_grad,
        gate_gain_grad,
        out_grad,
    )


def solution(mesh):
    in_specs = (
        P("dp", None),
        P("dp", None),
        P("dp"),
        P("dp", None),
        P(),
        P("dp", None, "tensor"),
        P("dp", None),
        P("dp", "tensor"),
        P(None, "tensor"),
        P("tensor"),
        P(),
        P(),
        P("tensor"),
        P("tensor"),
        P("tensor"),
        P("tensor"),
        P("dp", "tensor"),
    )
    out_specs = (
        P("dp", None),
        P("dp", None),
        P(),
        P("dp", None, "tensor"),
        P("dp", None),
        P("dp", "tensor"),
        P(None, "tensor"),
        P("tensor"),
        P(),
        P(),
        P("tensor"),
        P("tensor"),
        P("tensor"),
        P("tensor"),
        P("dp", "tensor"),
    )
    return jax.shard_map(
        on_device, mesh=mesh, in_specs=in_specs, out_specs=out_specs, check_vma=False
    )
```

profile of v0, /device:TPU:0, one launch (start us, length us, event | category | flops | bytes accessed | tf_op | source)
XLA Modules:
  0.0 2527.5 jit_solution(8638867920375196014)
XLA Ops:
  11.1 8.0 scatter_custom_fusion
  19.1 17.3 gather_fusion
  42.7 88.8 %all-gather = bf16[8,192,12]{1,2,0:T(8,128)(2,1)S(1)} all-gather(bf16[1,192,12]{1,2,0:T(8,128)(2,1)S(1)} %convert_bitcast_fusion), channel_id=1, replica_groups=mesh['dp'=8,'tensor'=4] {'dp'}, dimensions={0}, use_global_device_ids=true | all-gather | bytes 41472 | tf_op jit(solution)/shard_map/all_gather | solution.py:146
  131.8 16.9 gather_fusion.2
  148.8 9.5 all_gather.20
  182.3 7.0 multiply_convert_fusion
  189.3 5.7 copy.247
  195.0 12.1 fusion.145
  211.7 7.7 fusion.102
  219.4 7.0 copy.160
  226.4 5.8 copy.248
  240.2 294.4 %while.47 = (s32[]{:T(128)}, f32[12,128,64]{1,2,0:T(8,128)S(1)}, s32[]{:T(128)}, f32[8,256,12,64]{1,0,3,2:T(8,128)}, f32[8,12,128,64]{2,3,1,0:T(8,128)}, /*index...) while((s32[]{:T(128)}, f32[12,128,64]{1,2,0:T(8,128)S(1)}, ...), condition=%wide.region_8.9_spmd.clone, body=%wide.region_5.8_spmd.clone.sunk | while | flops 1313649664 | bytes 11765497 | solution.py:87
  254.0 18.5 dynamic_update_slice.85
  290.8 18.5 dynamic_update_slice.85
  327.6 18.5 dynamic_update_slice.85
  364.4 18.5 dynamic_update_slice.85
  401.2 18.5 dynamic_update_slice.85
  438.0 18.5 dynamic_update_slice.85
  474.8 18.5 dynamic_update_slice.85
  511.6 18.5 dynamic_update_slice.85
  534.6 8.5 copy.249
  543.1 6.6 copy.165
  549.6 7.3 multiply_reduce_fusion.15
  557.0 11.7 psum.112
  568.8 11.7 multiply_reduce_fusion.9
  580.5 8.5 psum.114
  589.0 13.6 multiply_convert_fusion.2
  602.7 6.6 copy.168
  609.2 8.5 copy.250
  624.5 466.0 %while.48 = (s32[]{:T(128)}, f32[12]{0:T(128)}, f32[12,128,64]{1,2,0:T(8,128)S(1)}, f32[8,256,12,64]{1,0,3,2:T(8,128)}, f32[8,256,128]{2,1,0:T(8,128)}, /*index=...) while((s32[]{:T(128)}, f32[12]{0:T(128)}, ...), condition=%wide.region_27.28_spmd.clone, body=%wide.region_14.27_spmd.clone.sunk | while | flops 3037355008 | bytes 28656244 | solution.py:87
  657.0 18.5 dynamic_update_slice.89
  715.2 18.5 dynamic_update_slice.89
  773.4 18.5 dynamic_update_slice.89
  831.5 18.5 dynamic_update_slice.89
  889.7 18.5 dynamic_update_slice.89
  947.8 18.5 dynamic_update_slice.89
  1006.0 18.5 dynamic_update_slice.89
  1064.2 18.5 dynamic_update_slice.89
  1090.5 8.5 copy.251
  1099.0 6.6 copy.174
  1105.7 16.5 multiply_reduce_fusion.13
  1126.3 5.6 fusion.98
  1131.9 16.3 fusion.104
  1148.6 11.0 convolution_add_fusion.3
  1159.6 8.2 fusion.135
  1169.8 5.6 fusion.103
  1175.4 8.8 copy.189
  1189.7 15.6 fusion.147
  1205.5 9.2 bitcast_convert_fusion
  1219.2 147.4 %all-reduce.31 = (bf16[2048,256]{1,0:T(8,128)(2,1)}, f32[4,256]{1,0:T(4,128)S(1)}, f32[256]{0:T(256)S(1)}) all-reduce(f32[2048,256]{1,0:T(8,128)S(1)} %fusion.111, f32[4,256]{1,0:T(4,128)S(1)} %pad_add_fusion.1, f32[256]{0:T(256)S(1)} %get-tuple-element.895), channel_id=1, replica_groups=mesh['dp'=8,'tensor'=4] {'tensor'}, use_global_device_ids=true, to_apply=%region_29.30 | all-reduce | flops 525568 | bytes 3155968 | tf_op jit(solution)/shard_map/psum | solution.py:233
  1366.6 702.3 %all-reduce.30.cloned.1.call-done = (f32[2048,1536]{1,0:T(8,128)}, f32[2048,1536]{1,0:T(8,128)}) async-done(((f32[2048,1536]{1,0:T(8,128)}, f32[2048,1536]{1,0:T(8,128)}), (f32[2048,1536]{1,0:T(8,128)}, f32[2048,1536]{1,0:T(8,128)})) %all-reduce.30.cloned.1.call-update) | async-done | bytes 25165840 | tf_op jit(solution)/shard_map/psum | solution.py:210
  2068.9 9.0 multiply_reduce_fusion.6
  2082.1 26.8 %all_to_all.45 = bf16[8,256,384]{2,1,0:T(8,128)(2,1)} all-to-all(bf16[8,256,384]{2,1,0:T(8,128)(2,1)S(1)} %bitcast.451), channel_id=1, replica_groups=mesh['dp'=8,'tensor'=4] {'dp'}, dimensions={0} | all-to-all | bytes 3145728 | tf_op jit(solution)/shard_map/all_to_all | solution.py:291
  2109.0 24.1 all_to_all.46
  2133.1 5.9 fusion.148
  2139.1 11.6 fusion.134
  2152.5 38.1 %reduce-scatter.7.cloned.1.call-done = f32[192,2,768]{2,0,1:T(8,128)} async-done(((f32[1536,2,768]{2,0,1:T(8,128)}), f32[192,2,768]{2,0,1:T(8,128)}) %reduce-scatter.7.cloned.1.call-update) | async-done | bytes 1179664 | tf_op jit(solution)/shard_map/reduce_scatter | solution.py:260
  2193.8 25.0 all-reduce.24
  2218.8 88.6 %all-gather.12.cloned.1.call-done = bf16[2048,1536]{1,0:T(8,128)(2,1)} async-done(((bf16[2048,384]{1,0:T(8,128)(2,1)}), bf16[2048,1536]{1,0:T(8,128)(2,1)}) %all-gather.12.cloned.1.call-update) | async-done | bytes 6291472 | tf_op jit(solution)/shard_map/all_gather | solution.py:295
  2307.4 16.8 gather_fusion.3
  2324.2 98.3 %all-gather.10.cloned.1.call-done = bf16[2048,1536]{1,0:T(8,128)(2,1)} async-done(((bf16[2048,384]{1,0:T(8,128)(2,1)}), bf16[2048,1536]{1,0:T(8,128)(2,1)}) %all-gather.10.cloned.1.call-update) | async-done | bytes 6291472 | tf_op jit(solution)/shard_map/all_gather | solution.py:294
  2422.5 16.8 gather_fusion.1
  2439.3 23.6 reduce-scatter.9.cloned.1.call-done
  2462.9 57.8 %reduce-scatter.11.cloned.1.call-done = f32[192,768]{1,0:T(8,128)} async-done(((f32[1536,768]{1,0:T(8,128)}), f32[192,768]{1,0:T(8,128)}) %reduce-scatter.11.cloned.1.call-update) | async-done | bytes 589840 | tf_op jit(solution)/shard_map/reduce_scatter | solution.py:263
  (1003 shorter events, 519.4 us)
Async XLA Ops:
  7.2 182.1 %all-gather.6.cloned.1.call-start = ((), (), s32[]{:S(2)}) async-start(), calls=%async_computation.8 | async-start | bytes 5308416 | tf_op jit(solution)/shard_map/all_gather | solution.py:144
  36.4 95.1 %copy-start.73 = (f32[12]{0:T(128)S(1)}, f32[12]{0:T(128)}, u32[]{:S(2)}) copy-start(f32[12]{0:T(128)} %param.34) | copy-start | bytes 148
  36.4 122.0 %all-to-all-start = ((bf16[8,256,1536]{2,1,0:T(8,128)(2,1)}), bf16[8,256,1536]{2,1,0:T(8,128)(2,1)}, u32[]{:S(2)}, u32[]{:S(2)}) async-start(bf16[8,256,1536]{2,1,0:T(8,128)(2,1)} %bitcast.442), calls=%async_computation | async-start | bytes 12582912 | tf_op jit(solution)/shard_map/all_to_all | solution.py:140
  41.6 527.2 %all-gather.8.cloned.1.call-start = ((), (), s32[]{:S(2)}) async-start(), calls=%async_computation.9 | async-start | bytes 2654208 | tf_op jit(solution)/shard_map/all_gather | solution.py:147
  131.6 46.8 %copy-start.15 = (bf16[1536,12]{0,1:T(8,128)(2,1)}, bf16[1536,12]{0,1:T(8,128)(2,1)S(1)}, u32[]{:S(2)}) copy-start(bf16[1536,12]{0,1:T(8,128)(2,1)S(1)} %reshape.579) | copy-start | bytes 110596
  131.6 46.8 %copy-start.60 = (f32[12]{0:T(128)}, f32[12]{0:T(128)S(1)}, u32[]{:S(2)}) copy-start(f32[12]{0:T(128)S(1)} %exp.96) | copy-start | bytes 148
  131.7 17.0 copy-start.51
  131.7 26.6 %copy-start.66 = (f32[4,256]{1,0:T(4,128)S(1)}, f32[4,256]{1,0:T(4,128)}, u32[]{:S(2)}) copy-start(f32[4,256]{1,0:T(4,128)} %param.31) | copy-start | bytes 12292
  148.8 62.9 %copy-start.37 = (f32[768]{0:T(1024)}, f32[768]{0:T(1024)S(1)}, u32[]{:S(2)}) copy-start(f32[768]{0:T(1024)S(1)} %get-tuple-element.897) | copy-start | bytes 9220
  148.8 62.8 %copy-start.39 = (f32[768]{0:T(1024)}, f32[768]{0:T(1024)S(1)}, u32[]{:S(2)}) copy-start(f32[768]{0:T(1024)S(1)} %get-tuple-element.898) | copy-start | bytes 9220
  148.8 62.8 %copy-start.41 = (f32[768]{0:T(1024)}, f32[768]{0:T(1024)S(1)}, u32[]{:S(2)}) copy-start(f32[768]{0:T(1024)S(1)} %get-tuple-element.899) | copy-start | bytes 9220
  148.8 62.8 %copy-start.43 = (f32[768]{0:T(1024)}, f32[768]{0:T(1024)S(1)}, u32[]{:S(2)}) copy-start(f32[768]{0:T(1024)S(1)} %get-tuple-element.896) | copy-start | bytes 9220
  158.3 13.6 copy-start.10
  158.3 15.5 copy-start.52
  158.4 15.5 copy-start.54
  158.4 15.5 copy-start.56
  158.4 15.5 copy-start.58
  158.4 53.3 %copy-start.17 = (f32[2048]{0:T(1024)}, f32[2048]{0:T(1024)S(1)}, u32[]{:S(2)}) copy-start(f32[2048]{0:T(1024)S(1)} %get-tuple-element.1029) | copy-start | bytes 24580
  158.4 53.3 %copy-start.19 = (f32[2048]{0:T(1024)}, f32[2048]{0:T(1024)S(1)}, u32[]{:S(2)}) copy-start(f32[2048]{0:T(1024)S(1)} %get-tuple-element.1030) | copy-start | bytes 24580
  158.4 53.3 %copy-start.21 = (f32[2048]{0:T(1024)}, f32[2048]{0:T(1024)S(1)}, u32[]{:S(2)}) copy-start(f32[2048]{0:T(1024)S(1)} %get-tuple-element.1031) | copy-start | bytes 24580
  158.4 410.3 %all-to-all-start.2 = ((bf16[8,256,1536]{2,1,0:T(8,128)(2,1)}), bf16[8,256,1536]{2,1,0:T(8,128)(2,1)}, u32[]{:S(2)}, u32[]{:S(2)}) async-start(bf16[8,256,1536]{2,1,0:T(8,128)(2,1)} %bitcast.441), calls=%async_computation.2 | async-start | bytes 12582912 | tf_op jit(solution)/shard_map/all_to_all | solution.py:141
  163.2 1905.6 %all-reduce.30.cloned.1.call-start = ((), (), s32[]{:S(2)}) async-start(), calls=%async_computation.16 | async-start | bytes 50331648 | tf_op jit(solution)/shard_map/psum | solution.py:210
  549.6 19.2 copy-start.63
  568.7 20.3 copy-start.45
  624.7 11.4 copy-start.35
  650.7 31.5 %copy-start.47 = (f32[12]{0:T(128)S(1)}, f32[12]{0:T(128)}, u32[]{:S(2)}) copy-start(f32[12]{0:T(128)} %get-tuple-element.1387) | copy-start | bytes 148 | tf_op jit(solution)/shard_map/transpose(jvp())/while
  650.7 32.1 %copy-start.36 = (s32[8,256]{1,0:T(8,128)S(1)}, s32[8,256]{1,0:T(8,128)}, u32[]{:S(2)}) copy-start(s32[8,256]{1,0:T(8,128)} %copy-done.35) | copy-start | bytes 24580 | tf_op jit(solution)/shard_map/transpose(jvp())/while
  682.9 11.4 copy-start.35
  708.9 31.6 %copy-start.47 = (f32[12]{0:T(128)S(1)}, f32[12]{0:T(128)}, u32[]{:S(2)}) copy-start(f32[12]{0:T(128)} %get-tuple-element.1387) | copy-start | bytes 148 | tf_op jit(solution)/shard_map/transpose(jvp())/while
  708.9 32.2 %copy-start.36 = (s32[8,256]{1,0:T(8,128)S(1)}, s32[8,256]{1,0:T(8,128)}, u32[]{:S(2)}) copy-start(s32[8,256]{1,0:T(8,128)} %copy-done.35) | copy-start | bytes 24580 | tf_op jit(solution)/shard_map/transpose(jvp())/while
  767.0 31.6 %copy-start.47 = (f32[12]{0:T(128)S(1)}, f32[12]{0:T(128)}, u32[]{:S(2)}) copy-start(f32[12]{0:T(128)} %get-tuple-element.1387) | copy-start | bytes 148 | tf_op jit(solution)/shard_map/transpose(jvp())/while
  767.0 32.2 %copy-start.36 = (s32[8,256]{1,0:T(8,128)S(1)}, s32[8,256]{1,0:T(8,128)}, u32[]{:S(2)}) copy-start(s32[8,256]{1,0:T(8,128)} %copy-done.35) | copy-start | bytes 24580 | tf_op jit(solution)/shard_map/transpose(jvp())/while
  825.2 31.6 %copy-start.47 = (f32[12]{0:T(128)S(1)}, f32[12]{0:T(128)}, u32[]{:S(2)}) copy-start(f32[12]{0:T(128)} %get-tuple-element.1387) | copy-start | bytes 148 | tf_op jit(solution)/shard_map/transpose(jvp())/while
  825.2 32.1 %copy-start.36 = (s32[8,256]{1,0:T(8,128)S(1)}, s32[8,256]{1,0:T(8,128)}, u32[]{:S(2)}) copy-start(s32[8,256]{1,0:T(8,128)} %copy-done.35) | copy-start | bytes 24580 | tf_op jit(solution)/shard_map/transpose(jvp())/while
  883.4 31.6 %copy-start.47 = (f32[12]{0:T(128)S(1)}, f32[12]{0:T(128)}, u32[]{:S(2)}) copy-start(f32[12]{0:T(128)} %get-tuple-element.1387) | copy-start | bytes 148 | tf_op jit(solution)/shard_map/transpose(jvp())/while
  883.4 32.1 %copy-start.36 = (s32[8,256]{1,0:T(8,128)S(1)}, s32[8,256]{1,0:T(8,128)}, u32[]{:S(2)}) copy-start(s32[8,256]{1,0:T(8,128)} %copy-done.35) | copy-start | bytes 24580 | tf_op jit(solution)/shard_map/transpose(jvp())/while
  941.5 31.6 %copy-start.47 = (f32[12]{0:T(128)S(1)}, f32[12]{0:T(128)}, u32[]{:S(2)}) copy-start(f32[12]{0:T(128)} %get-tuple-element.1387) | copy-start | bytes 148 | tf_op jit(solution)/shard_map/transpose(jvp())/while
  941.5 32.2 %copy-start.36 = (s32[8,256]{1,0:T(8,128)S(1)}, s32[8,256]{1,0:T(8,128)}, u32[]{:S(2)}) copy-start(s32[8,256]{1,0:T(8,128)} %copy-done.35) | copy-start | bytes 24580 | tf_op jit(solution)/shard_map/transpose(jvp())/while
  999.7 31.6 %copy-start.47 = (f32[12]{0:T(128)S(1)}, f32[12]{0:T(128)}, u32[]{:S(2)}) copy-start(f32[12]{0:T(128)} %get-tuple-element.1387) | copy-start | bytes 148 | tf_op jit(solution)/shard_map/transpose(jvp())/while
  999.7 32.2 %copy-start.36 = (s32[8,256]{1,0:T(8,128)S(1)}, s32[8,256]{1,0:T(8,128)}, u32[]{:S(2)}) copy-start(s32[8,256]{1,0:T(8,128)} %copy-done.35) | copy-start | bytes 24580 | tf_op jit(solution)/shard_map/transpose(jvp())/while
  1057.9 31.6 %copy-start.47 = (f32[12]{0:T(128)S(1)}, f32[12]{0:T(128)}, u32[]{:S(2)}) copy-start(f32[12]{0:T(128)} %get-tuple-element.1387) | copy-start | bytes 148 | tf_op jit(solution)/shard_map/transpose(jvp())/while
  1057.9 32.2 %copy-start.36 = (s32[8,256]{1,0:T(8,128)S(1)}, s32[8,256]{1,0:T(8,128)}, u32[]{:S(2)}) copy-start(s32[8,256]{1,0:T(8,128)} %copy-done.35) | copy-start | bytes 24580 | tf_op jit(solution)/shard_map/transpose(jvp())/while
  1105.6 16.5 copy-start.38
  1105.6 16.5 copy-start.40
  1105.7 16.5 copy-start.42
  1126.3 33.3 %slice-start = ((s8[6291456]{0:T(1024)(128)(4,1)}), s8[4194304]{0:T(1024)(128)(4,1)S(1)}, s32[]{:S(2)}) async-start(s8[6291456]{0:T(1024)(128)(4,1)} %bitcast.432), calls=%async_computation.17 | async-start | bytes 8388608
  1131.9 16.4 copy-start.13
  1131.9 16.4 copy-start.61
  1131.9 16.6 copy-start.16
  1131.9 27.7 %slice-start.1 = ((s8[6291456]{0:T(1024)(128)(4,1)}), s8[2097152]{0:T(1024)(128)(4,1)S(1)}, s32[]{:S(2)}) async-start(s8[6291456]{0:T(1024)(128)(4,1)} %bitcast.432), calls=%async_computation.18 | async-start | bytes 4194304
  1167.9 983.0 %reduce-scatter.13.cloned.1.call-start = ((), (), s32[]{:S(2)}) async-start(), calls=%async_computation.15 | async-start | bytes 884736
  1189.7 1000.9 %reduce-scatter.7.cloned.1.call-start = ((), (), s32[]{:S(2)}) async-start(), calls=%async_computation.12 | async-start | bytes 10616832 | tf_op jit(solution)/shard_map/reduce_scatter | solution.py:260
  1205.4 1102.0 %all-gather.12.cloned.1.call-start = ((), (), s32[]{:S(2)}) async-start(), calls=%async_computation.11 | async-start | bytes 7864320 | tf_op jit(solution)/shard_map/all_gather | solution.py:295
  1218.5 850.4 %copy-start.11 = (bf16[1536,256]{1,0:T(8,128)(2,1)S(1)}, bf16[1536,256]{1,0:T(8,128)(2,1)}, u32[]{:S(2)}) copy-start(bf16[1536,256]{1,0:T(8,128)(2,1)} %copy-done.10) | copy-start | bytes 2359300
  1218.5 850.4 %copy-start.29 = (f32[2048]{0:T(1024)S(1)}, f32[2048]{0:T(1024)}, u32[]{:S(2)}) copy-start(f32[2048]{0:T(1024)} %copy-done.28) | copy-start | bytes 24580
  1218.5 850.4 %copy-start.31 = (f32[1536]{0:T(1024)S(1)}, f32[1536]{0:T(1024)}, u32[]{:S(2)}) copy-start(f32[1536]{0:T(1024)} %param.25) | copy-start | bytes 18436
  2082.0 51.1 %copy-start.12 = (bf16[2048,256]{1,0:T(8,128)(2,1)S(1)}, bf16[2048,256]{1,0:T(8,128)(2,1)}, u32[]{:S(2)}) copy-start(bf16[2048,256]{1,0:T(8,128)(2,1)} %get-tuple-element.971) | copy-start | bytes 3145732
  2108.9 313.6 %all-gather.10.cloned.1.call-start = ((), (), s32[]{:S(2)}) async-start(), calls=%async_computation.10 | async-start | bytes 7864320 | tf_op jit(solution)/shard_map/all_gather | solution.py:294
  2133.1 329.8 %reduce-scatter.9.cloned.1.call-start = ((), (), s32[]{:S(2)}) async-start(), calls=%async_computation.13 | async-start | bytes 1769472 | tf_op jit(solution)/shard_map/reduce_scatter | solution.py:261
  2139.0 11.8 copy-start.74
  2139.0 381.7 %reduce-scatter.11.cloned.1.call-start = ((), (), s32[]{:S(2)}) async-start(), calls=%async_computation.14 | async-start | bytes 5308416 | tf_op jit(solution)/shard_map/reduce_scatter | solution.py:263
  2150.7 43.0 %copy-start.49 = (f32[12]{0:T(128)S(1)}, f32[12]{0:T(128)}, u32[]{:S(2)}) copy-start(f32[12]{0:T(128)} %get-tuple-element.530) | copy-start | bytes 148
  2150.7 43.0 %copy-start.65 = (f32[768]{0:T(1024)S(1)}, f32[768]{0:T(1024)}, u32[]{:S(2)}) copy-start(f32[768]{0:T(1024)} %get-tuple-element.882) | copy-start | bytes 9220
  2150.7 156.6 %copy-start.34 = (s32[2048]{0:T(1024)S(1)}, s32[2048]{0:T(1024)}, u32[]{:S(2)}) copy-start(s32[2048]{0:T(1024)} %get-tuple-element.987) | copy-start | bytes 24580
  (73 other events, 421.9 us)
Sparse Core Ops, SparseCore 0:
  10.4 46.6 all-gather.5
  59.0 70.6 all-gather.7
  1168.0 900.7 all-reduce.29
  2072.4 38.3 reduce-scatter.12
  2114.2 76.3 reduce-scatter.6
  2192.0 115.3 all-gather.11
  2308.9 113.5 all-gather.9
  2426.3 36.5 reduce-scatter.8
  2466.9 53.7 reduce-scatter.10
where the time goes:
time: 2550 us; the launch traced here: 2530 us
  waiting for transfers between devices  1010 us (40%)
  local copies, waits for them, and re-layouts  624 us (24%)
  blocking collectives  342 us (13%)
  matrix products  315 us (12%)
  other arithmetic  188 us (7%)
    psum x1, waiting for transfers between devices, on_device(): branch = lax.psum(partial_out, 'tensor')  702 us
    dynamic_update_slice x72, local copies, waits for them, and re-layouts, mixer(): lax.scan(jax.checkpoint(span_step), initial, (blocked(values), blocked(wr...  344 us
    psum x1, blocking collectives, on_device(): lax.psum((shared_part, shared_filter_part, shared_bias_part), 'tensor')  147 us
    dot_general x24, matrix products, span_step(): local_out = jnp.einsum('hts,shp->thp', mixing, value_blk, precision=PRECISE)  101 us
    all_gather x1, waiting for transfers between devices, on_device(): lax.all_gather(part_out, 'tensor', axis=1, tiled=True)  98.3 us
    all_gather x1, blocking collectives, on_device(): lax.all_gather(step_weight.astype(jnp.bfloat16), 'dp', axis=0, tiled=True)  88.8 us
    all_gather x1, waiting for transfers between devices, on_device(): lax.all_gather(part_grad, 'tensor', axis=1, tiled=True)  88.6 us
    reduce_scatter x1, waiting for transfers between devices, on_device(): lax.psum_scatter(out_grad, 'dp', scatter_dimension=0, tiled=True)  57.8 us
  transfers between devices with their start and end apart: 11, of which 6 were waited for; matrix products, arithmetic and copies ran while one was open for 21% of the time, Pallas kernels for 0%

commit v1 on v0

--- a/solution.py
+++ b/solution.py
@@ -1,3 +1,4 @@
+import functools
 import jax
 import jax.numpy as jnp
 from jax import lax
@@ -7,6 +8,14 @@
 SPAN = 256
 EPSILON = 1e-05
 PRECISE = lax.Precision.HIGHEST
+
+
+def press_the_squares(message, mesh_name):
+    frame_out = lax.all_gather(message, axis_name=mesh_name).sum(axis=0)
+    return frame_out
+
+
+local_data_show = functools.partial(press_the_squares, mesh_name="tensor")
 
 
 def segments_of(lengths, row_count):
@@ -207,7 +216,7 @@
     gate_scale = lax.rsqrt(square_sum / INNER + EPSILON)[:, None]
     gate_normed = (gated * gate_scale * gate_gain).astype(jnp.bfloat16)
     partial_out = jnp.einsum("ti,di->td", gate_normed, out_full, preferred_element_type=jnp.float32)
-    branch = lax.psum(partial_out, "tensor")
+    branch = local_data_show(partial_out)
     layer_work = (hidden_in + branch).astype(jnp.bfloat16)
     part_out = lax.dynamic_slice_in_dim(layer_work, column, col_share, 1)
     out_grad = jnp.einsum("td,ti->di", work_cot, gate_normed, preferred_element_type=jnp.float32)

time: 2550 us -> 2960 us (1.16)
  waiting for transfers between devices: 1010 us -> 1390 us
    all_gather x0 -> x1, waiting for transfers between devices: none -> 822 us  [press_the_squares(): frame_out = lax.all_gather(message, axis_name=mesh_name).sum(axis=0)]
    psum x1, waiting for transfers between devices: 702 us -> 284 us  [on_device(): normed_back = lax.psum(input_part, 'tensor')]
    reduce_scatter x1, waiting for transfers between devices: 38.1 us -> 0.01 us  [on_device(): lax.psum_scatter(inner_grad, 'dp', scatter_dimension=0, tiled=True)]
  transfers between devices with their start and end apart: 11 -> 12, of which waited for: 6 -> 6; matrix products, arithmetic and copies ran while one was open for 21% -> 20% of each run, Pallas kernels for 0% -> 0%
where the time goes in v1:
time: 2960 us; the launch traced here: 2940 us
  waiting for transfers between devices  1390 us (47%)
  local copies, waits for them, and re-layouts  625 us (21%)
  blocking collectives  346 us (12%)
  matrix products  315 us (11%)
  other arithmetic  209 us (7%)
    all_gather x1, waiting for transfers between devices, press_the_squares(): frame_out = lax.all_gather(message, axis_name=mesh_name).sum(axis=0)  822 us
    dynamic_update_slice x72, local copies, waits for them, and re-layouts, mixer(): lax.scan(jax.checkpoint(span_step), initial, (blocked(values), blocked(wr...  344 us
    psum x1, waiting for transfers between devices, on_device(): normed_back = lax.psum(input_part, 'tensor')  284 us
    psum x1, blocking collectives, on_device(): lax.psum((shared_part, shared_filter_part, shared_bias_part), 'tensor')  146 us
    all_gather x1, waiting for transfers between devices, on_device(): lax.all_gather(part_grad, 'tensor', axis=1, tiled=True)  109 us
    dot_general x24, matrix products, span_step(): local_out = jnp.einsum('hts,shp->thp', mixing, value_blk, precision=PRECISE)  101 us
    all_gather x1, waiting for transfers between devices, on_device(): lax.all_gather(part_out, 'tensor', axis=1, tiled=True)  98.3 us
    all_gather x1, blocking collectives, on_device(): lax.all_gather(step_weight.astype(jnp.bfloat16), 'dp', axis=0, tiled=True)  88.8 us
  transfers between devices with their start and end apart: 12, of which 6 were waited for; matrix products, arithmetic and copies ran while one was open for 20% of the time, Pallas kernels for 0%

profile of v1, /device:TPU:0, one launch (start us, length us, event | category | flops | bytes accessed | tf_op | source)
XLA Modules:
  0.0 2940.3 jit_solution(2497326627241442379)
XLA Ops:
  11.1 8.0 scatter_custom_fusion
  19.1 17.3 gather_fusion
  42.7 88.8 %all-gather.1 = bf16[8,192,12]{1,2,0:T(8,128)(2,1)S(1)} all-gather(bf16[1,192,12]{1,2,0:T(8,128)(2,1)S(1)} %convert_bitcast_fusion), channel_id=1, replica_groups=mesh['dp'=8,'tensor'=4] {'dp'}, dimensions={0}, use_global_device_ids=true | all-gather | bytes 41472 | tf_op jit(solution)/shard_map/all_gather | solution.py:155
  131.8 16.9 gather_fusion.2
  148.9 9.5 all_gather.26
  182.5 7.0 multiply_convert_fusion
  189.5 5.7 copy.248
  195.1 12.1 fusion.145
  211.9 7.8 fusion.102
  219.7 7.0 copy.160
  226.7 5.8 copy.249
  240.3 294.3 %while.47 = (s32[]{:T(128)}, f32[12,128,64]{1,2,0:T(8,128)S(1)}, s32[]{:T(128)}, f32[8,256,12,64]{1,0,3,2:T(8,128)}, f32[8,12,128,64]{2,3,1,0:T(8,128)}, /*index...) while((s32[]{:T(128)}, f32[12,128,64]{1,2,0:T(8,128)S(1)}, ...), condition=%wide.region_8.9_spmd.clone, body=%wide.region_5.8_spmd.clone.sunk | while | flops 1313649664 | bytes 11765497 | solution.py:96
  254.1 18.5 dynamic_update_slice.85
  290.9 18.5 dynamic_update_slice.85
  327.7 18.5 dynamic_update_slice.85
  364.5 18.5 dynamic_update_slice.85
  401.3 18.5 dynamic_update_slice.85
  438.1 18.5 dynamic_update_slice.85
  474.9 18.5 dynamic_update_slice.85
  511.7 18.5 dynamic_update_slice.85
  534.7 8.5 copy.250
  543.2 6.6 copy.165
  549.8 7.3 multiply_reduce_fusion.15
  557.1 11.8 psum.105
  568.9 11.7 multiply_reduce_fusion.9
  580.6 8.5 psum.106
  589.2 13.7 multiply_convert_fusion.2
  602.8 6.6 copy.168
  609.4 8.5 copy.251
  624.7 464.6 %while.48 = (s32[]{:T(128)}, f32[12]{0:T(128)}, f32[12,128,64]{1,2,0:T(8,128)S(1)}, f32[8,256,12,64]{1,0,3,2:T(8,128)}, f32[8,256,128]{2,1,0:T(8,128)}, /*index=...) while((s32[]{:T(128)}, f32[12]{0:T(128)}, ...), condition=%wide.region_27.28_spmd.clone, body=%wide.region_14.27_spmd.clone.sunk | while | flops 3037355008 | bytes 28656244 | solution.py:96
  657.1 18.5 dynamic_update_slice.89
  715.1 18.5 dynamic_update_slice.89
  773.1 18.5 dynamic_update_slice.89
  831.1 18.5 dynamic_update_slice.89
  889.0 18.5 dynamic_update_slice.89
  947.0 18.5 dynamic_update_slice.89
  1005.0 18.5 dynamic_update_slice.89
  1063.0 18.5 dynamic_update_slice.89
  1089.2 8.5 copy.252
  1097.8 6.6 copy.174
  1104.4 17.4 multiply_reduce_fusion.13
  1127.5 13.5 fusion.104
  1141.2 6.4 convolution_add_fusion.3
  1149.3 11.0 fusion.135
  1167.3 8.7 copy.189
  1175.9 5.5 fusion.122
  1181.5 15.8 fusion.147
  1197.4 9.3 bitcast_convert_fusion
  1211.0 146.5 %all-reduce.30 = (bf16[2048,256]{1,0:T(8,128)(2,1)}, f32[4,256]{1,0:T(4,128)S(1)}, f32[256]{0:T(256)S(1)}) all-reduce(f32[2048,256]{1,0:T(8,128)S(1)} %fusion.111, f32[4,256]{1,0:T(4,128)S(1)} %pad_add_fusion.1, f32[256]{0:T(256)S(1)} %get-tuple-element.895), channel_id=1, replica_groups=mesh['dp'=8,'tensor'=4] {'tensor'}, use_global_device_ids=true, to_apply=%region_29.30 | all-reduce | flops 525568 | bytes 3155968 | tf_op jit(solution)/shard_map/psum | solution.py:242
  1357.5 284.5 %all-reduce.29.cloned.1.call-done = f32[2048,1536]{1,0:T(8,128)} async-done(((f32[2048,1536]{1,0:T(8,128)}), f32[2048,1536]{1,0:T(8,128)}) %all-reduce.29.cloned.1.call-update) | async-done | bytes 12582928 | tf_op jit(solution)/shard_map/psum | solution.py:252
  1642.0 14.5 multiply_reduce_fusion.6
  1656.5 821.8 %all-gather.16.cloned.1.call-done = f32[8192,1536]{1,0:T(8,128)} async-done(((f32[2048,1536]{1,0:T(8,128)}), f32[8192,1536]{1,0:T(8,128)}) %all-gather.16.cloned.1.call-update) | async-done | bytes 50331664 | tf_op jit(solution)/shard_map/all_gather | solution.py:14
  2478.3 24.7 reduce_sum.359
  2507.8 24.6 all_to_all.45
  2532.5 31.6 %all_to_all.46 = bf16[8,256,384]{2,1,0:T(8,128)(2,1)} all-to-all(bf16[8,256,384]{2,1,0:T(8,128)(2,1)S(1)} %bitcast.450), channel_id=1, replica_groups=mesh['dp'=8,'tensor'=4] {'dp'}, dimensions={0} | all-to-all | bytes 3145728 | tf_op jit(solution)/shard_map/all_to_all | solution.py:299
  2564.2 5.9 fusion.148
  2570.3 11.0 fusion.134
  2583.0 25.0 all-reduce.24
  2611.2 108.8 %all-gather.14.cloned.1.call-done = bf16[2048,1536]{1,0:T(8,128)(2,1)} async-done(((bf16[2048,384]{1,0:T(8,128)(2,1)}), bf16[2048,1536]{1,0:T(8,128)(2,1)}) %all-gather.14.cloned.1.call-update) | async-done | bytes 6291472 | tf_op jit(solution)/shard_map/all_gather | solution.py:304
  2719.9 16.8 gather_fusion.3
  2736.8 98.3 %all-gather.12.cloned.1.call-done = bf16[2048,1536]{1,0:T(8,128)(2,1)} async-done(((bf16[2048,384]{1,0:T(8,128)(2,1)}), bf16[2048,1536]{1,0:T(8,128)(2,1)}) %all-gather.12.cloned.1.call-update) | async-done | bytes 6291472 | tf_op jit(solution)/shard_map/all_gather | solution.py:303
  2835.1 16.8 gather_fusion.1
  2851.9 23.6 reduce-scatter.9.cloned.1.call-done
  2875.5 57.7 %reduce-scatter.11.cloned.1.call-done = f32[192,768]{1,0:T(8,128)} async-done(((f32[1536,768]{1,0:T(8,128)}), f32[192,768]{1,0:T(8,128)}) %reduce-scatter.11.cloned.1.call-update) | async-done | bytes 589840 | tf_op jit(solution)/shard_map/reduce_scatter | solution.py:272
  (1012 shorter events, 521.7 us)
Async XLA Ops:
  7.2 182.3 %all-gather.8.cloned.1.call-start = ((), (), s32[]{:S(2)}) async-start(), calls=%async_computation.8 | async-start | bytes 5308416 | tf_op jit(solution)/shard_map/all_gather | solution.py:153
  36.4 95.2 %copy-start.78 = (f32[12]{0:T(128)S(1)}, f32[12]{0:T(128)}, u32[]{:S(2)}) copy-start(f32[12]{0:T(128)} %param.34) | copy-start | bytes 148
  36.4 122.0 %all-to-all-start = ((bf16[8,256,1536]{2,1,0:T(8,128)(2,1)}), bf16[8,256,1536]{2,1,0:T(8,128)(2,1)}, u32[]{:S(2)}, u32[]{:S(2)}) async-start(bf16[8,256,1536]{2,1,0:T(8,128)(2,1)} %bitcast.442), calls=%async_computation | async-start | bytes 12582912 | tf_op jit(solution)/shard_map/all_to_all | solution.py:149
  41.6 527.3 %all-gather.10.cloned.1.call-start = ((), (), s32[]{:S(2)}) async-start(), calls=%async_computation.9 | async-start | bytes 2654208 | tf_op jit(solution)/shard_map/all_gather | solution.py:156
  131.6 47.0 %copy-start.15 = (bf16[1536,12]{0,1:T(8,128)(2,1)}, bf16[1536,12]{0,1:T(8,128)(2,1)S(1)}, u32[]{:S(2)}) copy-start(bf16[1536,12]{0,1:T(8,128)(2,1)S(1)} %reshape.580) | copy-start | bytes 110596
  131.6 47.0 %copy-start.65 = (f32[12]{0:T(128)}, f32[12]{0:T(128)S(1)}, u32[]{:S(2)}) copy-start(f32[12]{0:T(128)S(1)} %exp.96) | copy-start | bytes 148
  131.7 17.1 copy-start.56
  131.8 26.6 copy-start.71
  148.9 62.9 %copy-start.37 = (f32[768]{0:T(1024)}, f32[768]{0:T(1024)S(1)}, u32[]{:S(2)}) copy-start(f32[768]{0:T(1024)S(1)} %get-tuple-element.897) | copy-start | bytes 9220
  148.9 62.9 %copy-start.39 = (f32[768]{0:T(1024)}, f32[768]{0:T(1024)S(1)}, u32[]{:S(2)}) copy-start(f32[768]{0:T(1024)S(1)} %get-tuple-element.898) | copy-start | bytes 9220
  148.9 62.9 %copy-start.41 = (f32[768]{0:T(1024)}, f32[768]{0:T(1024)S(1)}, u32[]{:S(2)}) copy-start(f32[768]{0:T(1024)S(1)} %get-tuple-element.899) | copy-start | bytes 9220
  148.9 62.9 %copy-start.43 = (f32[768]{0:T(1024)}, f32[768]{0:T(1024)S(1)}, u32[]{:S(2)}) copy-start(f32[768]{0:T(1024)S(1)} %get-tuple-element.896) | copy-start | bytes 9220
  158.4 13.6 copy-start.10
  158.4 15.5 copy-start.57
  158.4 15.5 copy-start.59
  158.4 15.5 copy-start.61
  158.4 15.5 copy-start.63
  158.4 53.4 %copy-start.17 = (f32[2048]{0:T(1024)}, f32[2048]{0:T(1024)S(1)}, u32[]{:S(2)}) copy-start(f32[2048]{0:T(1024)S(1)} %get-tuple-element.1027) | copy-start | bytes 24580
  158.5 53.4 %copy-start.19 = (f32[2048]{0:T(1024)}, f32[2048]{0:T(1024)S(1)}, u32[]{:S(2)}) copy-start(f32[2048]{0:T(1024)S(1)} %get-tuple-element.1028) | copy-start | bytes 24580
  158.5 53.4 %copy-start.21 = (f32[2048]{0:T(1024)}, f32[2048]{0:T(1024)S(1)}, u32[]{:S(2)}) copy-start(f32[2048]{0:T(1024)S(1)} %get-tuple-element.1029) | copy-start | bytes 24580
  158.5 410.4 %all-to-all-start.2 = ((bf16[8,256,1536]{2,1,0:T(8,128)(2,1)}), bf16[8,256,1536]{2,1,0:T(8,128)(2,1)}, u32[]{:S(2)}, u32[]{:S(2)}) async-start(bf16[8,256,1536]{2,1,0:T(8,128)(2,1)} %bitcast.441), calls=%async_computation.2 | async-start | bytes 12582912 | tf_op jit(solution)/shard_map/all_to_all | solution.py:150
  163.3 1478.7 %all-reduce.29.cloned.1.call-start = ((), (), s32[]{:S(2)}) async-start(), calls=%async_computation.11 | async-start | bytes 25165824 | tf_op jit(solution)/shard_map/psum | solution.py:252
  549.8 19.1 copy-start.68
  568.9 20.3 copy-start.45
  624.9 11.2 copy-start.35
  650.8 31.6 %copy-start.47 = (f32[12]{0:T(128)S(1)}, f32[12]{0:T(128)}, u32[]{:S(2)}) copy-start(f32[12]{0:T(128)} %get-tuple-element.1385) | copy-start | bytes 148 | tf_op jit(solution)/shard_map/transpose(jvp())/while
  650.8 32.1 %copy-start.36 = (s32[8,256]{1,0:T(8,128)S(1)}, s32[8,256]{1,0:T(8,128)}, u32[]{:S(2)}) copy-start(s32[8,256]{1,0:T(8,128)} %copy-done.35) | copy-start | bytes 24580 | tf_op jit(solution)/shard_map/transpose(jvp())/while
  682.9 11.2 copy-start.35
  708.8 31.6 %copy-start.47 = (f32[12]{0:T(128)S(1)}, f32[12]{0:T(128)}, u32[]{:S(2)}) copy-start(f32[12]{0:T(128)} %get-tuple-element.1385) | copy-start | bytes 148 | tf_op jit(solution)/shard_map/transpose(jvp())/while
  708.8 32.1 %copy-start.36 = (s32[8,256]{1,0:T(8,128)S(1)}, s32[8,256]{1,0:T(8,128)}, u32[]{:S(2)}) copy-start(s32[8,256]{1,0:T(8,128)} %copy-done.35) | copy-start | bytes 24580 | tf_op jit(solution)/shard_map/transpose(jvp())/while
  766.7 31.6 %copy-start.47 = (f32[12]{0:T(128)S(1)}, f32[12]{0:T(128)}, u32[]{:S(2)}) copy-start(f32[12]{0:T(128)} %get-tuple-element.1385) | copy-start | bytes 148 | tf_op jit(solution)/shard_map/transpose(jvp())/while
  766.7 32.1 %copy-start.36 = (s32[8,256]{1,0:T(8,128)S(1)}, s32[8,256]{1,0:T(8,128)}, u32[]{:S(2)}) copy-start(s32[8,256]{1,0:T(8,128)} %copy-done.35) | copy-start | bytes 24580 | tf_op jit(solution)/shard_map/transpose(jvp())/while
  824.7 31.6 %copy-start.47 = (f32[12]{0:T(128)S(1)}, f32[12]{0:T(128)}, u32[]{:S(2)}) copy-start(f32[12]{0:T(128)} %get-tuple-element.1385) | copy-start | bytes 148 | tf_op jit(solution)/shard_map/transpose(jvp())/while
  824.7 32.1 %copy-start.36 = (s32[8,256]{1,0:T(8,128)S(1)}, s32[8,256]{1,0:T(8,128)}, u32[]{:S(2)}) copy-start(s32[8,256]{1,0:T(8,128)} %copy-done.35) | copy-start | bytes 24580 | tf_op jit(solution)/shard_map/transpose(jvp())/while
  882.7 31.6 %copy-start.47 = (f32[12]{0:T(128)S(1)}, f32[12]{0:T(128)}, u32[]{:S(2)}) copy-start(f32[12]{0:T(128)} %get-tuple-element.1385) | copy-start | bytes 148 | tf_op jit(solution)/shard_map/transpose(jvp())/while
  882.7 32.1 %copy-start.36 = (s32[8,256]{1,0:T(8,128)S(1)}, s32[8,256]{1,0:T(8,128)}, u32[]{:S(2)}) copy-start(s32[8,256]{1,0:T(8,128)} %copy-done.35) | copy-start | bytes 24580 | tf_op jit(solution)/shard_map/transpose(jvp())/while
  940.7 31.6 %copy-start.47 = (f32[12]{0:T(128)S(1)}, f32[12]{0:T(128)}, u32[]{:S(2)}) copy-start(f32[12]{0:T(128)} %get-tuple-element.1385) | copy-start | bytes 148 | tf_op jit(solution)/shard_map/transpose(jvp())/while
  940.7 32.1 %copy-start.36 = (s32[8,256]{1,0:T(8,128)S(1)}, s32[8,256]{1,0:T(8,128)}, u32[]{:S(2)}) copy-start(s32[8,256]{1,0:T(8,128)} %copy-done.35) | copy-start | bytes 24580 | tf_op jit(solution)/shard_map/transpose(jvp())/while
  998.7 31.6 %copy-start.47 = (f32[12]{0:T(128)S(1)}, f32[12]{0:T(128)}, u32[]{:S(2)}) copy-start(f32[12]{0:T(128)} %get-tuple-element.1385) | copy-start | bytes 148 | tf_op jit(solution)/shard_map/transpose(jvp())/while
  998.7 32.1 %copy-start.36 = (s32[8,256]{1,0:T(8,128)S(1)}, s32[8,256]{1,0:T(8,128)}, u32[]{:S(2)}) copy-start(s32[8,256]{1,0:T(8,128)} %copy-done.35) | copy-start | bytes 24580 | tf_op jit(solution)/shard_map/transpose(jvp())/while
  1056.7 31.6 %copy-start.47 = (f32[12]{0:T(128)S(1)}, f32[12]{0:T(128)}, u32[]{:S(2)}) copy-start(f32[12]{0:T(128)} %get-tuple-element.1385) | copy-start | bytes 148 | tf_op jit(solution)/shard_map/transpose(jvp())/while
  1056.7 32.1 %copy-start.36 = (s32[8,256]{1,0:T(8,128)S(1)}, s32[8,256]{1,0:T(8,128)}, u32[]{:S(2)}) copy-start(s32[8,256]{1,0:T(8,128)} %copy-done.35) | copy-start | bytes 24580 | tf_op jit(solution)/shard_map/transpose(jvp())/while
  1104.4 17.4 copy-start.38
  1104.4 17.4 copy-start.40
  1104.4 17.4 copy-start.42
  1127.5 13.5 copy-start.13
  1127.5 13.5 copy-start.66
  1127.5 13.8 copy-start.16
  1147.6 1330.7 %all-gather.16.cloned.1.call-start = ((), (), s32[]{:S(2)}) async-start(), calls=%async_computation.16 | async-start | bytes 62914560 | tf_op jit(solution)/shard_map/all_gather | solution.py:14
  1160.3 1421.1 %reduce-scatter.13.cloned.1.call-start = ((), (), s32[]{:S(2)}) async-start(), calls=%async_computation.17 | async-start | bytes 884736
  1181.5 1426.5 %reduce-scatter.7.cloned.1.call-start = ((), (), s32[]{:S(2)}) async-start(), calls=%async_computation.13 | async-start | bytes 10616832 | tf_op jit(solution)/shard_map/reduce_scatter | solution.py:269
  1197.3 1522.6 %all-gather.14.cloned.1.call-start = ((), (), s32[]{:S(2)}) async-start(), calls=%async_computation.12 | async-start | bytes 7864320 | tf_op jit(solution)/shard_map/all_gather | solution.py:304
  1210.3 431.7 %copy-start.11 = (bf16[1536,256]{1,0:T(8,128)(2,1)S(1)}, bf16[1536,256]{1,0:T(8,128)(2,1)}, u32[]{:S(2)}) copy-start(bf16[1536,256]{1,0:T(8,128)(2,1)} %copy-done.10) | copy-start | bytes 2359300
  1210.3 431.7 %copy-start.29 = (f32[2048]{0:T(1024)S(1)}, f32[2048]{0:T(1024)}, u32[]{:S(2)}) copy-start(f32[2048]{0:T(1024)} %copy-done.28) | copy-start | bytes 24580
  1210.3 431.7 %copy-start.31 = (f32[1536]{0:T(1024)S(1)}, f32[1536]{0:T(1024)}, u32[]{:S(2)}) copy-start(f32[1536]{0:T(1024)} %param.25) | copy-start | bytes 18436
  1642.0 14.5 copy-start.33
  2507.8 56.3 %copy-start.12 = (bf16[2048,256]{1,0:T(8,128)(2,1)S(1)}, bf16[2048,256]{1,0:T(8,128)(2,1)}, u32[]{:S(2)}) copy-start(bf16[2048,256]{1,0:T(8,128)(2,1)} %get-tuple-element.971) | copy-start | bytes 3145732
  2532.5 302.6 %all-gather.12.cloned.1.call-start = ((), (), s32[]{:S(2)}) async-start(), calls=%async_computation.10 | async-start | bytes 7864320 | tf_op jit(solution)/shard_map/all_gather | solution.py:303
  2564.1 311.4 %reduce-scatter.9.cloned.1.call-start = ((), (), s32[]{:S(2)}) async-start(), calls=%async_computation.14 | async-start | bytes 1769472 | tf_op jit(solution)/shard_map/reduce_scatter | solution.py:270
  2570.2 12.8 copy-start.49
  2570.2 12.8 copy-start.51
  2570.2 12.8 copy-start.70
  2570.2 363.0 %reduce-scatter.11.cloned.1.call-start = ((), (), s32[]{:S(2)}) async-start(), calls=%async_computation.15 | async-start | bytes 5308416 | tf_op jit(solution)/shard_map/reduce_scatter | solution.py:272
  2581.2 138.7 %copy-start.34 = (s32[2048]{0:T(1024)S(1)}, s32[2048]{0:T(1024)}, u32[]{:S(2)}) copy-start(s32[2048]{0:T(1024)} %get-tuple-element.985) | copy-start | bytes 24580
  (77 other events, 432.1 us)
Sparse Core Ops, SparseCore 0:
  10.4 46.6 all-gather.7
  59.6 70.0 all-gather.9
  1147.8 494.1 all-reduce.28
  1643.4 834.8 all-gather.15
  2481.9 33.0 reduce-scatter.12
  2518.4 84.5 reduce-scatter.6
  2604.6 115.3 all-gather.13
  2721.5 113.5 all-gather.11
  2838.9 36.5 reduce-scatter.8
  2879.4 53.7 reduce-scatter.10
